TPU v7x, 32 devices: a whole 2x2x4 slice. The times are simulated.
32 devices in a mesh: clips: 2 (over y), row: 4 (over x, core), col: 4 (over z).
Axes of the slice: x: 2, y: 2, z: 4, core: 2. Of those that a mesh axis runs over, the one named last changes fastest.
Arguments:
- clip_tokens: bfloat16 [2048, 6144], P(('clips', 'col'), 'row'), parts along dimension 0, may hold values from -12 to 12
- modulation: float32 [8, 6, 6144], P('clips', None, 'row'), parts along dimension 0, may hold values from -3 to 3
- w_qkv: bfloat16 [6144, 3, 4096], P('row', None, 'col'), may hold values from -3 to 3
- w_out: bfloat16 [4096, 6144], P('col', 'row'), may hold values from -0.09375 to 0.09375
- w_up: bfloat16 [6144, 12288], P('row', 'col'), may hold values from -0.078125 to 0.078125
- up_bias: float32 [12288], P('col'), may hold values from -3 to 3
- w_down: bfloat16 [12288, 6144], P('col', 'row'), may hold values from -0.0546875 to 0.0546875
- guide_num: int32 [8], P('clips'), parts along dimension 0, may hold values from -3 to 10, as said below
Outputs:
- guided: bfloat16 [512, 6144], P(('clips', 'col'), 'row'), parts along dimension 0
There are 2 independent parts, one for each index of `clips`. A program takes and returns all parts, laid end to end along the dimension named above; an argument that names none is the same for every part. Nothing has to cross between parts.
Inputs may be any that keep to these rules, and one draw needn't show every extreme that they name: `guide_num`: the three negative numerators are -1, -2 and -3 in some order, and the positive one makes the four sum to 4.
All inputs are finite; a program needn't handle non-finite values.
Results may differ from a plain program's by a relative error of at most 0.019.
Values may be sent and summed in bfloat16 or wider, within the bound.
A program may use at most 128 MiB of HBM per device.

v0:
```python
import jax
import jax.numpy as jnp
from jax import lax
from jax.sharding import PartitionSpec as P

D = 6144
HEAD_DIM = 128
eps = 1e-06


def normalize(values, shift, scale):
    totals = lax.psum((jnp.sum(values, axis=1), jnp.sum(values * values, axis=1)), "row")
    mean = totals[0] / D
    variance = totals[1] / D - mean * mean
    normed = (values - mean[:, None]) * lax.rsqrt(variance + eps)[:, None]
    branches = shift.shape[0]
    shaped = normed.reshape(-1, branches, values.shape[1]) * (1.0 + scale[None]) + shift[None]
    return shaped.reshape(values.shape)


def general_layer(clip_tokens, modulation, w_qkv, w_out, w_up, up_bias, w_down, guide_num):
    branches = modulation.shape[0]
    feat_rows = w_qkv.shape[0]
    head_cols = w_qkv.shape[2]
    heads_here = head_cols // HEAD_DIM
    x_rows = clip_tokens.astype(jnp.float32)
    first = normalize(x_rows, modulation[:, 0], modulation[:, 1]).astype(jnp.bfloat16)
    w_flat = w_qkv.reshape(feat_rows, 3 * head_cols)
    partial_qkv = jnp.dot(
        lax.all_gather(first, "col", axis=0, tiled=True), w_flat, preferred_element_type=jnp.float32
    )
    scale_score = 1.0 / jnp.sqrt(jnp.float32(HEAD_DIM))
    qkv = lax.psum_scatter(partial_qkv.astype(jnp.bfloat16), "row", scatter_dimension=0, tiled=True)
    query3 = qkv[:, :head_cols].reshape(-1, heads_here, HEAD_DIM)
    query_rows = query3.shape[0]
    piece = (
        lax.all_gather(qkv[:, head_cols : 2 * head_cols], "row", axis=0, tiled=True),
        lax.all_gather(qkv[:, 2 * head_cols :], "row", axis=0, tiled=True),
    )
    top = jnp.full((heads_here, query_rows), -1e30, jnp.float32)
    rows = piece[0].shape[0]
    key_heads = piece[0].reshape(rows, heads_here, HEAD_DIM)
    value_heads = piece[1].reshape(rows, heads_here, HEAD_DIM)
    scores = (
        jnp.einsum("qhd,khd->hqk", query3, key_heads, preferred_element_type=jnp.float32)
        * scale_score
    )
    query_branch = jnp.arange(query3.shape[0], dtype=jnp.int32) % branches
    key_branch = jnp.arange(rows, dtype=jnp.int32) % branches
    allowed = (query_branch[:, None] == key_branch[None, :])[None]
    masked = jnp.where(allowed, scores, -1e30)
    new_top = jnp.maximum(top, jnp.max(masked, axis=-1))
    weights = jnp.where(allowed, jnp.exp(masked - new_top[..., None]), 0.0)
    denom = jnp.sum(weights, axis=-1)
    accum = jnp.einsum(
        "hqk,khd->hqd",
        weights.astype(jnp.bfloat16),
        value_heads,
        preferred_element_type=jnp.float32,
    )
    att = (accum / denom[..., None]).transpose(1, 0, 2).reshape(-1, head_cols).astype(jnp.bfloat16)
    partial_out = jnp.dot(
        lax.all_gather(att, "row", axis=0, tiled=True), w_out, preferred_element_type=jnp.float32
    )
    out_rows = lax.psum_scatter(
        partial_out.astype(jnp.bfloat16), "col", scatter_dimension=0, tiled=True
    ).astype(jnp.float32)
    by_branch = x_rows.shape[0] // branches
    resid = (
        x_rows.reshape(by_branch, branches, feat_rows)
        + modulation[None, :, 2] * out_rows.reshape(by_branch, branches, feat_rows)
    ).reshape(x_rows.shape)
    second = normalize(resid, modulation[:, 3], modulation[:, 4]).astype(jnp.bfloat16)
    partial_up = jnp.dot(
        lax.all_gather(second, "col", axis=0, tiled=True), w_up, preferred_element_type=jnp.float32
    )
    up_rows = lax.psum_scatter(
        partial_up.astype(jnp.bfloat16), "row", scatter_dimension=0, tiled=True
    ).astype(jnp.float32)
    act = jax.nn.gelu(up_rows + up_bias[None], approximate=True).astype(jnp.bfloat16)
    partial_down = jnp.dot(
        lax.all_gather(act, "row", axis=0, tiled=True), w_down, preferred_element_type=jnp.float32
    )
    guide_weights = guide_num.astype(jnp.float32) / 4.0
    weights_gate = guide_weights[:, None] * modulation[:, 5]
    combined = jnp.sum(partial_down.reshape(-1, branches, feat_rows) * weights_gate[None], axis=1)
    mlp_rows = lax.psum_scatter(
        combined.astype(jnp.bfloat16), "col", scatter_dimension=0, tiled=True
    ).astype(jnp.float32)
    resid_mix = jnp.sum(
        resid.reshape(by_branch, branches, feat_rows) * guide_weights[None, :, None], axis=1
    )
    return (resid_mix + mlp_rows).astype(jnp.bfloat16)


BF = jnp.bfloat16


def swap_row(value, distance):
    size = lax.axis_size("row")
    return lax.ppermute(value, "row", [(r, r ^ distance) for r in range(size)])


def sum_over_row(value):
    value = value + swap_row(value, 1)
    return value + swap_row(value, 2)


def scatter_row(pieces):
    me = lax.axis_index("row")
    half, core = (me // 2, me % 2)
    mine = lax.dynamic_index_in_dim(pieces, core, 1, keepdims=False)
    theirs = lax.dynamic_index_in_dim(pieces, 1 - core, 1, keepdims=False)
    got = swap_row(theirs, 1)
    away = lax.dynamic_index_in_dim(mine, 1 - half, 0, keepdims=False).astype(
        jnp.float32
    ) + lax.dynamic_index_in_dim(got, 1 - half, 0, keepdims=False).astype(jnp.float32)
    came = swap_row(away.astype(BF), 2)
    kept = lax.dynamic_index_in_dim(mine, half, 0, keepdims=False).astype(
        jnp.float32
    ) + lax.dynamic_index_in_dim(got, half, 0, keepdims=False).astype(jnp.float32)
    return kept + came.astype(jnp.float32)


def gather_row(value):
    me = lax.axis_index("row")
    half, core = (me // 2, me % 2)
    other = swap_row(value, 2)
    pair = jnp.where(half == 0, jnp.stack([value, other]), jnp.stack([other, value]))
    beside = swap_row(pair, 1)
    return jnp.where(
        core == 0, jnp.stack([pair, beside], axis=1), jnp.stack([beside, pair], axis=1)
    )


def moments(values):
    return jnp.stack([jnp.sum(values, axis=1), jnp.sum(values * values, axis=1)])


def apply_norm(values, totals, shift, scale):
    mean = totals[0] / D
    variance = totals[1] / D - mean * mean
    normed = (values - mean[:, None]) * lax.rsqrt(variance + eps)[:, None]
    return (normed * (1.0 + scale[None]) + shift[None]).astype(BF)


def attend(q, k, v):
    scores = jnp.einsum("qhd,khd->hqk", q, k, preferred_element_type=jnp.float32)
    scores = scores / jnp.sqrt(jnp.float32(HEAD_DIM))
    weights = jnp.exp(scores - jnp.max(scores, axis=-1, keepdims=True))
    denom = jnp.sum(weights, axis=-1)
    mixed = jnp.einsum("hqk,khd->hqd", weights.astype(BF), v, preferred_element_type=jnp.float32)
    mixed = mixed / denom[..., None]
    return mixed.transpose(1, 0, 2).reshape(q.shape[0], -1).astype(BF)


def branch_layer(clip_tokens, modulation, w_qkv, w_out, w_up, up_bias, w_down, guide_num):
    branches = modulation.shape[0]
    feat_rows, _, head_cols = w_qkv.shape
    here = clip_tokens.shape[0] // branches
    w_flat = w_qkv.reshape(feat_rows, 3 * head_cols)
    by_branch = clip_tokens.reshape(here, branches, feat_rows).transpose(1, 0, 2)
    mine = head_cols // 4
    guide = guide_num.astype(jnp.float32) / 4.0
    total = None
    mixed = None
    for b in range(branches):
        x = by_branch[b]
        x_all = lax.all_gather(x, "col", axis=0, tiled=True).astype(jnp.float32)
        tokens = x_all.shape[0]
        first = apply_norm(x_all, sum_over_row(moments(x_all)), modulation[b, 0], modulation[b, 1])
        partial = jnp.dot(first, w_flat, preferred_element_type=jnp.float32).astype(BF)
        pieces = partial.reshape(tokens, 3, 2, 2, mine).transpose(2, 3, 1, 0, 4)
        qkv = scatter_row(pieces).astype(BF).reshape(3, tokens, mine // HEAD_DIM, HEAD_DIM)
        att = attend(qkv[0], qkv[1], qkv[2])
        att_all = gather_row(att).reshape(4, tokens, mine).transpose(1, 0, 2).reshape(tokens, -1)
        partial = jnp.dot(att_all, w_out, preferred_element_type=jnp.float32).astype(BF)
        out = lax.psum_scatter(partial, "col", scatter_dimension=0, tiled=True)
        resid = x.astype(jnp.float32) + modulation[b, 2][None] * out.astype(jnp.float32)
        second = apply_norm(resid, sum_over_row(moments(resid)), modulation[b, 3], modulation[b, 4])
        second_all = lax.all_gather(second, "col", axis=0, tiled=True)
        partial = jnp.dot(second_all, w_up, preferred_element_type=jnp.float32).astype(BF)
        up = scatter_row(partial.reshape(2, 2, tokens // 4, -1))
        act = jax.nn.gelu(up + up_bias[None], approximate=True).astype(BF)
        act_all = gather_row(act).reshape(tokens, -1)
        down = jnp.dot(act_all, w_down, preferred_element_type=jnp.float32)
        down = down * (guide[b] * modulation[b, 5])[None]
        total = down if total is None else total + down
        part = guide[b] * resid
        mixed = part if mixed is None else mixed + part
    mlp = lax.psum_scatter(total.astype(BF), "col", scatter_dimension=0, tiled=True)
    return (mixed + mlp.astype(jnp.float32)).astype(BF)


def on_device(*args):
    heads_here = args[2].shape[2] // HEAD_DIM
    if lax.axis_size("row") == 4 and heads_here % 4 == 0:
        return branch_layer(*args)
    return general_layer(*args)


def solution(mesh):
    in_specs = (
        P(("clips", "col"), "row"),
        P("clips", None, "row"),
        P("row", None, "col"),
        P("col", "row"),
        P("row", "col"),
        P("col"),
        P("col", "row"),
        P("clips"),
    )
    out_specs = P(("clips", "col"), "row")
    return jax.shard_map(
        on_device, mesh=mesh, in_specs=in_specs, out_specs=out_specs, check_vma=False
    )
```

profile of v0, /device:TPU:0, one launch (start us, length us, event | category | flops | bytes accessed | tf_op | source)
XLA Modules:
  0.0 575.6 jit_solution(8317175544174087421)
XLA Ops:
  10.4 21.3 %all-gather.3 = bf16[1,256,1536]{2,1,0:T(8,128)(2,1)S(1)} all-gather(bf16[1,64,1536]{2,1,0:T(8,128)(2,1)S(1)} %get-tuple-element.56), channel_id=5, replica_groups=mesh['clips'=2,'row'=4,'col'=4] {'col'}, dimensions={1}, use_global_device_ids=true | all-gather | bytes 983040 | tf_op jit(solution)/shard_map/all_gather | solution.py:169
  32.2 18.0 %all-gather.2 = bf16[1,256,1536]{2,1,0:T(8,128)(2,1)S(1)} all-gather(bf16[1,64,1536]{2,1,0:T(8,128)(2,1)S(1)} %get-tuple-element.55), channel_id=4, replica_groups=mesh['clips'=2,'row'=4,'col'=4] {'col'}, dimensions={1}, use_global_device_ids=true | all-gather | bytes 983040 | tf_op jit(solution)/shard_map/all_gather | solution.py:169
  51.1 18.1 %all-gather.1 = bf16[1,256,1536]{2,1,0:T(8,128)(2,1)S(1)} all-gather(bf16[1,64,1536]{2,1,0:T(8,128)(2,1)S(1)} %get-tuple-element.57), channel_id=3, replica_groups=mesh['clips'=2,'row'=4,'col'=4] {'col'}, dimensions={1}, use_global_device_ids=true | all-gather | bytes 983040 | tf_op jit(solution)/shard_map/all_gather | solution.py:169
  70.2 18.7 %all-gather = bf16[1,256,1536]{2,1,0:T(8,128)(2,1)S(1)} all-gather(bf16[1,64,1536]{2,1,0:T(8,128)(2,1)S(1)} %get-tuple-element.58), channel_id=2, replica_groups=mesh['clips'=2,'row'=4,'col'=4] {'col'}, dimensions={1}, use_global_device_ids=true | all-gather | bytes 983040 | tf_op jit(solution)/shard_map/all_gather | solution.py:169
  94.9 12.7 %copy.38 = bf16[1536,3,1024]{0,2,1:T(8,128)(2,1)} copy(bf16[1536,3,1024]{2,0,1:T(8,128)(2,1)} %param.10) | data formatting | bytes 18874368 | tf_op args[2]
  112.0 7.8 %convolution_convert_fusion.4 = bf16[256,3072]{1,0:T(8,128)(2,1)} fusion(bf16[1536,3072]{0,1:T(8,128)(2,1)} %bitcast.477, bf16[1,256,1536]{2,1,0:T(8,128)(2,1)} %copy-done.14, f32[1536]{0:T(1024)S(1)} %get-tuple-element.29, f32[1536]{0:T(1024)S(1)} %get-tuple-element.30, f32[256]{0:T(256)S(1)} %add_rsqrt_fusion, f32[256]{0:T(256)S(1)} %bitcast.609), kind=kOutput, calls=%fused_computation.4 | convolution fusion | flops 2419064832 | bytes 11810816 | tf_op jit(solution)/shard_map/dot_general | solution.py:172
  119.8 5.0 reshape.1011
  129.2 11.0 %convolution_convert_fusion.5 = bf16[256,3072]{1,0:T(8,128)(2,1)} fusion(bf16[1536,3072]{0,1:T(8,128)(2,1)} %bitcast.478, bf16[1,256,1536]{2,1,0:T(8,128)(2,1)S(1)} %copy-done.13, f32[1536]{0:T(1024)S(1)} %get-tuple-element.32, f32[1536]{0:T(1024)S(1)} %get-tuple-element.33, f32[256]{0:T(256)S(1)} %add_rsqrt_fusion.1, f32[256]{0:T(256)S(1)} %bitcast.611), kind=kOutput, calls=%fused_computation.5 | convolution fusion | flops 2419064832 | bytes 11810816 | tf_op jit(solution)/shard_map/dot_general | solution.py:172
  140.2 5.2 reshape.1009
  149.8 11.0 %convolution_convert_fusion.6 = bf16[256,3072]{1,0:T(8,128)(2,1)} fusion(bf16[1536,3072]{0,1:T(8,128)(2,1)} %bitcast.479, bf16[1,256,1536]{2,1,0:T(8,128)(2,1)S(1)} %copy-done.11, f32[1536]{0:T(1024)S(1)} %get-tuple-element.36, f32[1536]{0:T(1024)S(1)} %get-tuple-element.37, f32[256]{0:T(256)S(1)} %add_rsqrt_fusion.2, f32[256]{0:T(256)S(1)} %bitcast.613), kind=kOutput, calls=%fused_computation.6 | convolution fusion | flops 2419064832 | bytes 11810816 | tf_op jit(solution)/shard_map/dot_general | solution.py:172
  160.8 5.0 reshape.1007
  170.2 11.0 %convolution_convert_fusion.7 = bf16[256,3072]{1,0:T(8,128)(2,1)} fusion(bf16[1536,3072]{0,1:T(8,128)(2,1)} %bitcast.480, bf16[1,256,1536]{2,1,0:T(8,128)(2,1)S(1)} %copy-done.9, f32[1536]{0:T(1024)S(1)} %get-tuple-element.39, f32[1536]{0:T(1024)S(1)} %get-tuple-element.40, f32[256]{0:T(256)S(1)} %add_rsqrt_fusion.3, f32[256]{0:T(256)S(1)} %bitcast.607), kind=kOutput, calls=%fused_computation.7 | convolution fusion | flops 2419064832 | bytes 11810816 | tf_op jit(solution)/shard_map/dot_general | solution.py:172
  181.2 5.4 reshape.1005
  226.7 14.1 %collective-permute-done.22 = bf16[256,256]{1,0:T(8,128)(2,1)S(1)} collective-permute-done((bf16[256,256]{1,0:T(8,128)(2,1)}, bf16[256,256]{1,0:T(8,128)(2,1)S(1)}, u32[]{:S(2)}, u32[]{:S(2)}) %collective-permute-start.22) | collective-permute-done | bytes 131104 | tf_op jit(solution)/shard_map/ppermute | solution.py:101
  303.1 4.5 collective-permute-done.4
  317.3 8.5 %reduce-scatter.8.cloned.1.call-done = bf16[64,1536]{1,0:T(8,128)(2,1)} async-done(((bf16[256,1536]{1,0:T(8,128)(2,1)}), bf16[64,1536]{1,0:T(8,128)(2,1)}) %reduce-scatter.8.cloned.1.call-update) | async-done | bytes 196624 | tf_op jit(solution)/shard_map/reduce_scatter | solution.py:178
  325.9 24.8 %reduce-scatter.6.cloned.1.call-done = bf16[64,1536]{1,0:T(8,128)(2,1)} async-done(((bf16[256,1536]{1,0:T(8,128)(2,1)}), bf16[64,1536]{1,0:T(8,128)(2,1)}) %reduce-scatter.6.cloned.1.call-update) | async-done | bytes 196624 | tf_op jit(solution)/shard_map/reduce_scatter | solution.py:178
  361.7 18.1 %all_gather.31 = bf16[256,1536]{1,0:T(8,128)(2,1)S(1)} all-gather(bf16[64,1536]{1,0:T(8,128)(2,1)S(1)} %get-tuple-element.54), channel_id=1, replica_groups=mesh['clips'=2,'row'=4,'col'=4] {'col'}, dimensions={0}, use_global_device_ids=true | all-gather | bytes 983040 | tf_op jit(solution)/shard_map/all_gather | solution.py:181
  379.8 6.4 %convolution_convert_fusion = bf16[256,3072]{1,0:T(8,128)(2,1)S(1)} fusion(bf16[256,1536]{1,0:T(8,128)(2,1)S(1)} %all_gather.31, bf16[1536,3072]{1,0:T(8,128)(2,1)} %param.12), kind=kOutput, calls=%fused_computation | convolution fusion | flops 2416705536 | bytes 11796480 | tf_op jit(solution)/shard_map/dot_general | solution.py:182
  387.6 18.0 %all_gather.30 = bf16[256,1536]{1,0:T(8,128)(2,1)S(1)} all-gather(bf16[64,1536]{1,0:T(8,128)(2,1)S(1)} %get-tuple-element.52), channel_id=1, replica_groups=mesh['clips'=2,'row'=4,'col'=4] {'col'}, dimensions={0}, use_global_device_ids=true | all-gather | bytes 983040 | tf_op jit(solution)/shard_map/all_gather | solution.py:181
  408.4 18.2 %all_gather.29 = bf16[256,1536]{1,0:T(8,128)(2,1)S(1)} all-gather(bf16[64,1536]{1,0:T(8,128)(2,1)S(1)} %get-tuple-element.53), channel_id=1, replica_groups=mesh['clips'=2,'row'=4,'col'=4] {'col'}, dimensions={0}, use_global_device_ids=true | all-gather | bytes 983040 | tf_op jit(solution)/shard_map/all_gather | solution.py:181
  429.3 18.4 %all_gather.28 = bf16[256,1536]{1,0:T(8,128)(2,1)S(1)} all-gather(bf16[64,1536]{1,0:T(8,128)(2,1)S(1)} %get-tuple-element.51), channel_id=1, replica_groups=mesh['clips'=2,'row'=4,'col'=4] {'col'}, dimensions={0}, use_global_device_ids=true | all-gather | bytes 983040 | tf_op jit(solution)/shard_map/all_gather | solution.py:181
  455.2 7.4 %collective-permute-done.45 = bf16[64,3072]{1,0:T(8,128)(2,1)S(1)} collective-permute-done((bf16[64,3072]{1,0:T(8,128)(2,1)S(1)}, bf16[64,3072]{1,0:T(8,128)(2,1)S(1)}, u32[]{:S(2)}, u32[]{:S(2)}) %collective-permute-start.45) | collective-permute-done | bytes 393248 | tf_op jit(solution)/shard_map/ppermute | solution.py:101
  462.6 8.4 %collective-permute-done.39 = bf16[64,3072]{1,0:T(8,128)(2,1)S(1)} collective-permute-done((bf16[64,3072]{1,0:T(8,128)(2,1)S(1)}, bf16[64,3072]{1,0:T(8,128)(2,1)S(1)}, u32[]{:S(2)}, u32[]{:S(2)}) %collective-permute-start.39) | collective-permute-done | bytes 393248 | tf_op jit(solution)/shard_map/ppermute | solution.py:101
  471.0 8.4 %collective-permute-done.33 = bf16[64,3072]{1,0:T(8,128)(2,1)S(1)} collective-permute-done((bf16[64,3072]{1,0:T(8,128)(2,1)S(1)}, bf16[64,3072]{1,0:T(8,128)(2,1)S(1)}, u32[]{:S(2)}, u32[]{:S(2)}) %collective-permute-start.33) | collective-permute-done | bytes 393248 | tf_op jit(solution)/shard_map/ppermute | solution.py:101
  479.4 8.0 %collective-permute-done.27 = bf16[64,3072]{1,0:T(8,128)(2,1)S(1)} collective-permute-done((bf16[64,3072]{1,0:T(8,128)(2,1)S(1)}, bf16[64,3072]{1,0:T(8,128)(2,1)S(1)}, u32[]{:S(2)}, u32[]{:S(2)}) %collective-permute-start.27) | collective-permute-done | bytes 393248 | tf_op jit(solution)/shard_map/ppermute | solution.py:101
  493.2 8.0 %collective-permute-done.28 = bf16[64,3072]{1,0:T(8,128)(2,1)S(1)} collective-permute-done((bf16[64,3072]{1,0:T(8,128)(2,1)S(1)}, bf16[64,3072]{1,0:T(8,128)(2,1)S(1)}, u32[]{:S(2)}, u32[]{:S(2)}) %collective-permute-start.28) | collective-permute-done | bytes 393248 | tf_op jit(solution)/shard_map/ppermute | solution.py:101
  501.3 8.2 %collective-permute-done.34 = bf16[64,3072]{1,0:T(8,128)(2,1)S(1)} collective-permute-done((bf16[64,3072]{1,0:T(8,128)(2,1)S(1)}, bf16[64,3072]{1,0:T(8,128)(2,1)S(1)}, u32[]{:S(2)}, u32[]{:S(2)}) %collective-permute-start.34) | collective-permute-done | bytes 393248 | tf_op jit(solution)/shard_map/ppermute | solution.py:101
  509.8 8.2 %collective-permute-done.40 = bf16[64,3072]{1,0:T(8,128)(2,1)S(1)} collective-permute-done((bf16[64,3072]{1,0:T(8,128)(2,1)S(1)}, bf16[64,3072]{1,0:T(8,128)(2,1)S(1)}, u32[]{:S(2)}, u32[]{:S(2)}) %collective-permute-start.40) | collective-permute-done | bytes 393248 | tf_op jit(solution)/shard_map/ppermute | solution.py:101
  518.2 6.9 %collective-permute-done.46 = bf16[64,3072]{1,0:T(8,128)(2,1)S(1)} collective-permute-done((bf16[64,3072]{1,0:T(8,128)(2,1)S(1)}, bf16[64,3072]{1,0:T(8,128)(2,1)S(1)}, u32[]{:S(2)}, u32[]{:S(2)}) %collective-permute-start.46) | collective-permute-done | bytes 393248 | tf_op jit(solution)/shard_map/ppermute | solution.py:101
  541.6 22.3 %reduce-scatter.14.cloned.1.call-done = bf16[64,1536]{1,0:T(8,128)(2,1)} async-done(((bf16[256,1536]{1,0:T(8,128)(2,1)}), bf16[64,1536]{1,0:T(8,128)(2,1)}) %reduce-scatter.14.cloned.1.call-update) | async-done | bytes 196624 | tf_op jit(solution)/shard_map/reduce_scatter | solution.py:191
  563.9 4.9 add_convert_fusion
  (378 shorter events, 188.8 us)
Async XLA Ops:
  6.5 310.7 %reduce-scatter.12.cloned.1.call-start = ((), (), s32[]{:S(2)}) async-start(), calls=%async_computation.8 | async-start | bytes 983040 | tf_op jit(solution)/shard_map/reduce_scatter | solution.py:178
  32.1 75.4 %collective-permute-start.18 = (f32[2,256]{1,0:T(2,128)S(1)}, f32[2,256]{1,0:T(2,128)S(1)}, u32[]{:S(2)}, u32[]{:S(2)}) collective-permute-start(f32[2,256]{1,0:T(2,128)S(1)} %pad_maximum_fusion.3), channel_id=1, source_target_pairs={{0,4},{4,0},{8,12},{12,8},{1,5},{5,1},{9,13},{13,9},{2,6},{6,2},{1... | collective-permute-start | bytes 6152 | tf_op jit(solution)/shard_map/ppermute | solution.py:101
  50.6 58.5 %collective-permute-start.12 = (f32[2,256]{1,0:T(2,128)S(1)}, f32[2,256]{1,0:T(2,128)S(1)}, u32[]{:S(2)}, u32[]{:S(2)}) collective-permute-start(f32[2,256]{1,0:T(2,128)S(1)} %pad_maximum_fusion.2), channel_id=1, source_target_pairs={{0,4},{4,0},{8,12},{12,8},{1,5},{5,1},{9,13},{13,9},{2,6},{6,2},{1... | collective-permute-start | bytes 6152 | tf_op jit(solution)/shard_map/ppermute | solution.py:101
  69.7 40.0 %collective-permute-start.6 = (f32[2,256]{1,0:T(2,128)S(1)}, f32[2,256]{1,0:T(2,128)S(1)}, u32[]{:S(2)}, u32[]{:S(2)}) collective-permute-start(f32[2,256]{1,0:T(2,128)S(1)} %pad_maximum_fusion.1), channel_id=1, source_target_pairs={{0,4},{4,0},{8,12},{12,8},{1,5},{5,1},{9,13},{13,9},{2,6},{6,2},{1... | collective-permute-start | bytes 6152 | tf_op jit(solution)/shard_map/ppermute | solution.py:101
  90.1 21.3 %collective-permute-start = (f32[2,256]{1,0:T(2,128)S(1)}, f32[2,256]{1,0:T(2,128)S(1)}, u32[]{:S(2)}, u32[]{:S(2)}) collective-permute-start(f32[2,256]{1,0:T(2,128)S(1)} %pad_maximum_fusion), channel_id=1, source_target_pairs={{0,4},{4,0},{8,12},{12,8},{1,5},{5,1},{9,13},{13,9},{2,6},{6,2},{1... | collective-permute-start | bytes 6152 | tf_op jit(solution)/shard_map/ppermute | solution.py:101
  109.2 19.7 %collective-permute-start.13 = (f32[2,256]{1,0:T(2,128)S(1)}, f32[2,256]{1,0:T(2,128)S(1)}, u32[]{:S(2)}, u32[]{:S(2)}) collective-permute-start(f32[2,256]{1,0:T(2,128)S(1)} %fusion.152), channel_id=1, source_target_pairs={{0,8},{4,12},{8,0},{12,4},{1,9},{5,13},{9,1},{13,5},{2,10},{6,14},... | collective-permute-start | bytes 6152 | tf_op jit(solution)/shard_map/ppermute | solution.py:101
  109.8 40.0 %collective-permute-start.7 = (f32[2,256]{1,0:T(2,128)S(1)}, f32[2,256]{1,0:T(2,128)S(1)}, u32[]{:S(2)}, u32[]{:S(2)}) collective-permute-start(f32[2,256]{1,0:T(2,128)S(1)} %fusion.153), channel_id=1, source_target_pairs={{0,8},{4,12},{8,0},{12,4},{1,9},{5,13},{9,1},{13,5},{2,10},{6,14},... | collective-permute-start | bytes 6152 | tf_op jit(solution)/shard_map/ppermute | solution.py:101
  111.4 58.8 %collective-permute-start.1 = (f32[2,256]{1,0:T(2,128)S(1)}, f32[2,256]{1,0:T(2,128)S(1)}, u32[]{:S(2)}, u32[]{:S(2)}) collective-permute-start(f32[2,256]{1,0:T(2,128)S(1)} %fusion.154), channel_id=1, source_target_pairs={{0,8},{4,12},{8,0},{12,4},{1,9},{5,13},{9,1},{13,5},{2,10},{6,14},... | collective-permute-start | bytes 6152 | tf_op jit(solution)/shard_map/ppermute | solution.py:101
  128.9 71.4 %collective-permute-start.20 = (bf16[2,3,256,256]{3,2,1,0:T(8,128)(2,1)}, bf16[2,3,256,256]{3,2,1,0:T(8,128)(2,1)}, u32[]{:S(2)}, u32[]{:S(2)}) collective-permute-start(bf16[2,3,256,256]{3,2,1,0:T(8,128)(2,1)} %bitcast.467), channel_id=1, source_target_pairs={{0,4},{4,0},{8,12},{12,8},{1,5},{5,1},{9,13},{13,9},{2,6},{6,2},{1... | collective-permute-start | bytes 2359304 | tf_op jit(solution)/shard_map/ppermute | solution.py:101
  149.4 53.5 %collective-permute-start.14 = (bf16[2,3,256,256]{3,2,1,0:T(8,128)(2,1)}, bf16[2,3,256,256]{3,2,1,0:T(8,128)(2,1)}, u32[]{:S(2)}, u32[]{:S(2)}) collective-permute-start(bf16[2,3,256,256]{3,2,1,0:T(8,128)(2,1)} %bitcast.468), channel_id=1, source_target_pairs={{0,4},{4,0},{8,12},{12,8},{1,5},{5,1},{9,13},{13,9},{2,6},{6,2},{1... | collective-permute-start | bytes 2359304 | tf_op jit(solution)/shard_map/ppermute | solution.py:101
  169.9 35.4 %collective-permute-start.8 = (bf16[2,3,256,256]{3,2,1,0:T(8,128)(2,1)}, bf16[2,3,256,256]{3,2,1,0:T(8,128)(2,1)}, u32[]{:S(2)}, u32[]{:S(2)}) collective-permute-start(bf16[2,3,256,256]{3,2,1,0:T(8,128)(2,1)} %bitcast.469), channel_id=1, source_target_pairs={{0,4},{4,0},{8,12},{12,8},{1,5},{5,1},{9,13},{13,9},{2,6},{6,2},{1... | collective-permute-start | bytes 2359304 | tf_op jit(solution)/shard_map/ppermute | solution.py:101
  189.8 18.8 %collective-permute-start.2 = (bf16[2,3,256,256]{3,2,1,0:T(8,128)(2,1)S(1)}, bf16[2,3,256,256]{3,2,1,0:T(8,128)(2,1)S(1)}, u32[]{:S(2)}, u32[]{:S(2)}) collective-permute-start(bf16[2,3,256,256]{3,2,1,0:T(8,128)(2,1)S(1)} %bitcast.529), channel_id=1, source_target_pairs={{0,4},{4,0},{8,12},{12,8},{1,5},{5,1},{9,13},{13,9},{2,6},{6,2},{1... | collective-permute-start | bytes 2359304 | tf_op jit(solution)/shard_map/ppermute | solution.py:101
  204.8 20.4 %collective-permute-start.15 = (bf16[3,256,256]{2,1,0:T(8,128)(2,1)}, bf16[3,256,256]{2,1,0:T(8,128)(2,1)}, u32[]{:S(2)}, u32[]{:S(2)}) collective-permute-start(bf16[3,256,256]{2,1,0:T(8,128)(2,1)} %fusion.92), channel_id=1, source_target_pairs={{0,8},{4,12},{8,0},{12,4},{1,9},{5,13},{9,1},{13,5},{2,10},{6,14},... | collective-permute-start | bytes 1179656 | tf_op jit(solution)/shard_map/ppermute | solution.py:101
  207.2 53.0 %collective-permute-start.9 = (bf16[3,256,256]{2,1,0:T(8,128)(2,1)}, bf16[3,256,256]{2,1,0:T(8,128)(2,1)}, u32[]{:S(2)}, u32[]{:S(2)}) collective-permute-start(bf16[3,256,256]{2,1,0:T(8,128)(2,1)} %fusion.95), channel_id=1, source_target_pairs={{0,8},{4,12},{8,0},{12,4},{1,9},{5,13},{9,1},{13,5},{2,10},{6,14},... | collective-permute-start | bytes 1179656 | tf_op jit(solution)/shard_map/ppermute | solution.py:101
  209.6 73.4 %collective-permute-start.3 = (bf16[3,256,256]{2,1,0:T(8,128)(2,1)}, bf16[3,256,256]{2,1,0:T(8,128)(2,1)}, u32[]{:S(2)}, u32[]{:S(2)}) collective-permute-start(bf16[3,256,256]{2,1,0:T(8,128)(2,1)} %fusion.98), channel_id=1, source_target_pairs={{0,8},{4,12},{8,0},{12,4},{1,9},{5,13},{9,1},{13,5},{2,10},{6,14},... | collective-permute-start | bytes 1179656 | tf_op jit(solution)/shard_map/ppermute | solution.py:101
  222.8 18.0 %collective-permute-start.22 = (bf16[256,256]{1,0:T(8,128)(2,1)}, bf16[256,256]{1,0:T(8,128)(2,1)S(1)}, u32[]{:S(2)}, u32[]{:S(2)}) collective-permute-start(bf16[256,256]{1,0:T(8,128)(2,1)} %copy.101), channel_id=1, source_target_pairs={{0,8},{4,12},{8,0},{12,4},{1,9},{5,13},{9,1},{13,5},{2,10},{6,14},... | collective-permute-start | bytes 393224 | tf_op jit(solution)/shard_map/ppermute | solution.py:101
  252.8 64.5 %reduce-scatter.10.cloned.1.call-start = ((), (), s32[]{:S(2)}) async-start(), calls=%async_computation.7 | async-start | bytes 983040 | tf_op jit(solution)/shard_map/reduce_scatter | solution.py:178
  275.7 50.2 %reduce-scatter.8.cloned.1.call-start = ((), (), s32[]{:S(2)}) async-start(), calls=%async_computation.6 | async-start | bytes 983040 | tf_op jit(solution)/shard_map/reduce_scatter | solution.py:178
  299.7 51.0 %reduce-scatter.6.cloned.1.call-start = ((), (), s32[]{:S(2)}) async-start(), calls=%async_computation.5 | async-start | bytes 983040 | tf_op jit(solution)/shard_map/reduce_scatter | solution.py:178
  317.2 246.7 %reduce-scatter.14.cloned.1.call-start = ((), (), s32[]{:S(2)}) async-start(), calls=%async_computation.9 | async-start | bytes 983040 | tf_op jit(solution)/shard_map/reduce_scatter | solution.py:191
  386.4 64.1 %collective-permute-start.44 = (bf16[2,64,3072]{2,1,0:T(8,128)(2,1)S(1)}, bf16[2,64,3072]{2,1,0:T(8,128)(2,1)S(1)}, u32[]{:S(2)}, u32[]{:S(2)}) collective-permute-start(bf16[2,64,3072]{2,1,0:T(8,128)(2,1)S(1)} %dynamic-slice_bitcast_fusion), channel_id=1, source_target_pairs={{0,4},{4,0},{8,12},{12,8},{1,5},{5,1},{9,13},{13,9},{2,6},{6,2},{1... | collective-permute-start | bytes 2359304 | tf_op jit(solution)/shard_map/ppermute | solution.py:101
  408.3 42.8 %collective-permute-start.38 = (bf16[2,64,3072]{2,1,0:T(8,128)(2,1)S(1)}, bf16[2,64,3072]{2,1,0:T(8,128)(2,1)S(1)}, u32[]{:S(2)}, u32[]{:S(2)}) collective-permute-start(bf16[2,64,3072]{2,1,0:T(8,128)(2,1)S(1)} %dynamic-slice_bitcast_fusion.1), channel_id=1, source_target_pairs={{0,4},{4,0},{8,12},{12,8},{1,5},{5,1},{9,13},{13,9},{2,6},{6,2},{1... | collective-permute-start | bytes 2359304 | tf_op jit(solution)/shard_map/ppermute | solution.py:101
  429.2 23.6 %collective-permute-start.32 = (bf16[2,64,3072]{2,1,0:T(8,128)(2,1)S(1)}, bf16[2,64,3072]{2,1,0:T(8,128)(2,1)S(1)}, u32[]{:S(2)}, u32[]{:S(2)}) collective-permute-start(bf16[2,64,3072]{2,1,0:T(8,128)(2,1)S(1)} %dynamic-slice_bitcast_fusion.2), channel_id=1, source_target_pairs={{0,4},{4,0},{8,12},{12,8},{1,5},{5,1},{9,13},{13,9},{2,6},{6,2},{1... | collective-permute-start | bytes 2359304 | tf_op jit(solution)/shard_map/ppermute | solution.py:101
  451.2 19.8 %collective-permute-start.39 = (bf16[64,3072]{1,0:T(8,128)(2,1)S(1)}, bf16[64,3072]{1,0:T(8,128)(2,1)S(1)}, u32[]{:S(2)}, u32[]{:S(2)}) collective-permute-start(bf16[64,3072]{1,0:T(8,128)(2,1)S(1)} %fusion.80), channel_id=1, source_target_pairs={{0,8},{4,12},{8,0},{12,4},{1,9},{5,13},{9,1},{13,5},{2,10},{6,14},... | collective-permute-start | bytes 1179656 | tf_op jit(solution)/shard_map/ppermute | solution.py:101
  452.9 26.5 %collective-permute-start.33 = (bf16[64,3072]{1,0:T(8,128)(2,1)S(1)}, bf16[64,3072]{1,0:T(8,128)(2,1)S(1)}, u32[]{:S(2)}, u32[]{:S(2)}) collective-permute-start(bf16[64,3072]{1,0:T(8,128)(2,1)S(1)} %fusion.83), channel_id=1, source_target_pairs={{0,8},{4,12},{8,0},{12,4},{1,9},{5,13},{9,1},{13,5},{2,10},{6,14},... | collective-permute-start | bytes 1179656 | tf_op jit(solution)/shard_map/ppermute | solution.py:101
  453.6 33.8 %collective-permute-start.27 = (bf16[64,3072]{1,0:T(8,128)(2,1)S(1)}, bf16[64,3072]{1,0:T(8,128)(2,1)S(1)}, u32[]{:S(2)}, u32[]{:S(2)}) collective-permute-start(bf16[64,3072]{1,0:T(8,128)(2,1)S(1)} %fusion.86), channel_id=1, source_target_pairs={{0,8},{4,12},{8,0},{12,4},{1,9},{5,13},{9,1},{13,5},{2,10},{6,14},... | collective-permute-start | bytes 1179656 | tf_op jit(solution)/shard_map/ppermute | solution.py:101
  489.0 12.1 %collective-permute-start.28 = (bf16[64,3072]{1,0:T(8,128)(2,1)S(1)}, bf16[64,3072]{1,0:T(8,128)(2,1)S(1)}, u32[]{:S(2)}, u32[]{:S(2)}) collective-permute-start(bf16[64,3072]{1,0:T(8,128)(2,1)S(1)} %get-tuple-element.71), channel_id=1, source_target_pairs={{0,8},{4,12},{8,0},{12,4},{1,9},{5,13},{9,1},{13,5},{2,10},{6,14},... | collective-permute-start | bytes 1179656 | tf_op jit(solution)/shard_map/ppermute | solution.py:101
  489.6 20.0 %collective-permute-start.34 = (bf16[64,3072]{1,0:T(8,128)(2,1)S(1)}, bf16[64,3072]{1,0:T(8,128)(2,1)S(1)}, u32[]{:S(2)}, u32[]{:S(2)}) collective-permute-start(bf16[64,3072]{1,0:T(8,128)(2,1)S(1)} %get-tuple-element.72), channel_id=1, source_target_pairs={{0,8},{4,12},{8,0},{12,4},{1,9},{5,13},{9,1},{13,5},{2,10},{6,14},... | collective-permute-start | bytes 1179656 | tf_op jit(solution)/shard_map/ppermute | solution.py:101
  491.1 26.9 %collective-permute-start.40 = (bf16[64,3072]{1,0:T(8,128)(2,1)S(1)}, bf16[64,3072]{1,0:T(8,128)(2,1)S(1)}, u32[]{:S(2)}, u32[]{:S(2)}) collective-permute-start(bf16[64,3072]{1,0:T(8,128)(2,1)S(1)} %get-tuple-element.73), channel_id=1, source_target_pairs={{0,8},{4,12},{8,0},{12,4},{1,9},{5,13},{9,1},{13,5},{2,10},{6,14},... | collective-permute-start | bytes 1179656 | tf_op jit(solution)/shard_map/ppermute | solution.py:101
  491.6 33.5 %collective-permute-start.46 = (bf16[64,3072]{1,0:T(8,128)(2,1)S(1)}, bf16[64,3072]{1,0:T(8,128)(2,1)S(1)}, u32[]{:S(2)}, u32[]{:S(2)}) collective-permute-start(bf16[64,3072]{1,0:T(8,128)(2,1)S(1)} %get-tuple-element.74), channel_id=1, source_target_pairs={{0,8},{4,12},{8,0},{12,4},{1,9},{5,13},{9,1},{13,5},{2,10},{6,14},... | collective-permute-start | bytes 1179656 | tf_op jit(solution)/shard_map/ppermute | solution.py:101
  501.3 26.7 %collective-permute-start.29 = (bf16[2,64,3072]{2,1,0:T(8,128)(2,1)S(1)}, bf16[2,64,3072]{2,1,0:T(8,128)(2,1)S(1)}, u32[]{:S(2)}, u32[]{:S(2)}) collective-permute-start(bf16[2,64,3072]{2,1,0:T(8,128)(2,1)S(1)} %maximum_select_fusion.4), channel_id=1, source_target_pairs={{0,4},{4,0},{8,12},{12,8},{1,5},{5,1},{9,13},{13,9},{2,6},{6,2},{1... | collective-permute-start | bytes 2359304 | tf_op jit(solution)/shard_map/ppermute | solution.py:101
  509.7 16.2 %collective-permute-start.35 = (bf16[2,64,3072]{2,1,0:T(8,128)(2,1)S(1)}, bf16[2,64,3072]{2,1,0:T(8,128)(2,1)S(1)}, u32[]{:S(2)}, u32[]{:S(2)}) collective-permute-start(bf16[2,64,3072]{2,1,0:T(8,128)(2,1)S(1)} %maximum_select_fusion.6), channel_id=1, source_target_pairs={{0,4},{4,0},{8,12},{12,8},{1,5},{5,1},{9,13},{13,9},{2,6},{6,2},{1... | collective-permute-start | bytes 2359304 | tf_op jit(solution)/shard_map/ppermute | solution.py:101
  (74 other events, 1049.4 us)
Sparse Core Ops, SparseCore 0:
  252.9 23.0 reduce-scatter.11
  278.3 22.5 reduce-scatter.9
  303.3 22.5 reduce-scatter.7
  328.0 22.5 reduce-scatter.5
  541.7 22.1 reduce-scatter.13
where the time goes:
time: 580 us; the launch traced here: 576 us
  waiting for transfers between devices  151 us (26%)
  blocking collectives  149 us (26%)
  local copies, waits for them, and re-layouts  101 us (17%)
  matrix products  89.1 us (15%)
  other arithmetic  40.9 us (7%)
  starting transfers between devices  30 us (5%)
  between operations  14.7 us (3%)
    ppermute x48, waiting for transfers between devices, swap_row(): return lax.ppermute(value, 'row', [(r, r ^ distance) for r in range(size)])  95.6 us
    all_gather x4, blocking collectives, branch_layer(): x_all = lax.all_gather(x, 'col', axis=0, tiled=True).astype(jnp.float32)  76.1 us
    all_gather x4, blocking collectives, branch_layer(): second_all = lax.all_gather(second, 'col', axis=0, tiled=True)  72.7 us
    dot_general x4, matrix products, branch_layer(): jnp.dot(first, w_flat, preferred_element_type=jnp.float32).astype(BF)  40.9 us
    reduce_scatter x4, waiting for transfers between devices, branch_layer(): out = lax.psum_scatter(partial, 'col', scatter_dimension=0, tiled=True)  33.3 us
    ppermute x48, starting transfers between devices, swap_row(): return lax.ppermute(value, 'row', [(r, r ^ distance) for r in range(size)])  29.9 us
    reduce_scatter x1, waiting for transfers between devices, branch_layer(): lax.psum_scatter(total.astype(BF), 'col', scatter_dimension=0, tiled=True)  22.3 us
    unnamed x111, local copies, waits for them, and re-layouts  21.5 us
  transfers between devices with their start and end apart: 53, of which 22 were waited for; matrix products, arithmetic and copies ran while one was open for 34% of the time, Pallas kernels for 0%

commit v1 on v0

--- a/solution.py
+++ b/solution.py
@@ -6,6 +6,16 @@
 D = 6144
 HEAD_DIM = 128
 eps = 1e-06
+
+
+def pass_along(x, axis, d):
+    size = lax.axis_size(axis)
+    held, tiles = (x, [x])
+    for _ in range(size - 1):
+        held = lax.ppermute(held, axis, [(i, (i + 1) % size) for i in range(size)])
+        tiles.insert(0, held)
+    line = jnp.concatenate(tiles, axis=d)
+    return jnp.roll(line, (lax.axis_index(axis) + 1) * x.shape[d], axis=d)
 
 
 def normalize(values, shift, scale):
@@ -178,7 +188,7 @@
         out = lax.psum_scatter(partial, "col", scatter_dimension=0, tiled=True)
         resid = x.astype(jnp.float32) + modulation[b, 2][None] * out.astype(jnp.float32)
         second = apply_norm(resid, sum_over_row(moments(resid)), modulation[b, 3], modulation[b, 4])
-        second_all = lax.all_gather(second, "col", axis=0, tiled=True)
+        second_all = pass_along(second, "col", 0)
         partial = jnp.dot(second_all, w_up, preferred_element_type=jnp.float32).astype(BF)
         up = scatter_row(partial.reshape(2, 2, tokens // 4, -1))
         act = jax.nn.gelu(up + up_bias[None], approximate=True).astype(BF)

time: 580 us -> 563 us (0.971)
  blocking collectives: 149 us -> 76.1 us
  waiting for transfers between devices: 151 us -> 187 us
  matrix products: 89.1 us -> 101 us
    all_gather x4 -> x0, blocking collectives: 72.7 us -> none  [branch_layer(): second_all = lax.all_gather(second, 'col', axis=0, tiled=True)]
    ppermute x0 -> x12, waiting for transfers between devices: none -> 37.8 us  [pass_along(): held = lax.ppermute(held, axis, [(i, (i + 1) % size) for i in range(size)])]
    dot_general x4, matrix products: 14.2 us -> 25.6 us  [branch_layer(): jnp.dot(second_all, w_up, preferred_element_type=jnp.float32).astype(BF)]
    unnamed x111 -> x135, local copies, waits for them, and re-layouts: 21.5 us -> 23.2 us
  transfers between devices with their start and end apart: 53 -> 65, of which waited for: 22 -> 31; matrix products, arithmetic and copies ran while one was open for 34% -> 38% of each run, Pallas kernels for 0% -> 0%
where the time goes in v1:
time: 563 us; the launch traced here: 558 us
  waiting for transfers between devices  187 us (33%)
  local copies, waits for them, and re-layouts  102 us (18%)
  matrix products  101 us (18%)
  blocking collectives  76.1 us (14%)
  other arithmetic  41 us (7%)
  starting transfers between devices  35.3 us (6%)
  between operations  14.9 us (3%)
    ppermute x48, waiting for transfers between devices, swap_row(): return lax.ppermute(value, 'row', [(r, r ^ distance) for r in range(size)])  95.6 us
    all_gather x4, blocking collectives, branch_layer(): x_all = lax.all_gather(x, 'col', axis=0, tiled=True).astype(jnp.float32)  76.1 us
    dot_general x4, matrix products, branch_layer(): jnp.dot(first, w_flat, preferred_element_type=jnp.float32).astype(BF)  40.9 us
    ppermute x12, waiting for transfers between devices, pass_along(): held = lax.ppermute(held, axis, [(i, (i + 1) % size) for i in range(size)])  37.8 us
    reduce_scatter x4, waiting for transfers between devices, branch_layer(): out = lax.psum_scatter(partial, 'col', scatter_dimension=0, tiled=True)  33.2 us
    ppermute x48, starting transfers between devices, swap_row(): return lax.ppermute(value, 'row', [(r, r ^ distance) for r in range(size)])  30 us
    dot_general x4, matrix products, branch_layer(): jnp.dot(second_all, w_up, preferred_element_type=jnp.float32).astype(BF)  25.6 us
    unnamed x135, local copies, waits for them, and re-layouts  23.2 us
  transfers between devices with their start and end apart: 65, of which 31 were waited for; matrix products, arithmetic and copies ran while one was open for 38% of the time, Pallas kernels for 0%

profile of v1, /device:TPU:0, one launch (start us, length us, event | category | flops | bytes accessed | tf_op | source)
XLA Modules:
  0.0 557.9 jit_solution(15167379390504259466)
XLA Ops:
  10.4 21.3 %all-gather.3 = bf16[1,256,1536]{2,1,0:T(8,128)(2,1)S(1)} all-gather(bf16[1,64,1536]{2,1,0:T(8,128)(2,1)S(1)} %get-tuple-element.57), channel_id=5, replica_groups=mesh['clips'=2,'row'=4,'col'=4] {'col'}, dimensions={1}, use_global_device_ids=true | all-gather | bytes 983040 | tf_op jit(solution)/shard_map/all_gather | solution.py:179
  32.2 18.0 %all-gather.2 = bf16[1,256,1536]{2,1,0:T(8,128)(2,1)S(1)} all-gather(bf16[1,64,1536]{2,1,0:T(8,128)(2,1)S(1)} %get-tuple-element.56), channel_id=4, replica_groups=mesh['clips'=2,'row'=4,'col'=4] {'col'}, dimensions={1}, use_global_device_ids=true | all-gather | bytes 983040 | tf_op jit(solution)/shard_map/all_gather | solution.py:179
  51.1 18.1 %all-gather.1 = bf16[1,256,1536]{2,1,0:T(8,128)(2,1)S(1)} all-gather(bf16[1,64,1536]{2,1,0:T(8,128)(2,1)S(1)} %get-tuple-element.58), channel_id=3, replica_groups=mesh['clips'=2,'row'=4,'col'=4] {'col'}, dimensions={1}, use_global_device_ids=true | all-gather | bytes 983040 | tf_op jit(solution)/shard_map/all_gather | solution.py:179
  70.1 18.7 %all-gather = bf16[1,256,1536]{2,1,0:T(8,128)(2,1)S(1)} all-gather(bf16[1,64,1536]{2,1,0:T(8,128)(2,1)S(1)} %get-tuple-element.59), channel_id=2, replica_groups=mesh['clips'=2,'row'=4,'col'=4] {'col'}, dimensions={1}, use_global_device_ids=true | all-gather | bytes 983040 | tf_op jit(solution)/shard_map/all_gather | solution.py:179
  94.8 12.7 %copy.38 = bf16[1536,3,1024]{0,2,1:T(8,128)(2,1)} copy(bf16[1536,3,1024]{2,0,1:T(8,128)(2,1)} %param.12) | data formatting | bytes 18874368 | tf_op args[2]
  111.9 7.8 %convolution_convert_fusion.4 = bf16[256,3072]{1,0:T(8,128)(2,1)} fusion(bf16[1536,3072]{0,1:T(8,128)(2,1)} %bitcast.473, bf16[1,256,1536]{2,1,0:T(8,128)(2,1)} %copy-done.14, f32[1536]{0:T(1024)S(1)} %get-tuple-element.30, f32[1536]{0:T(1024)S(1)} %get-tuple-element.31, f32[256]{0:T(256)S(1)} %add_rsqrt_fusion, f32[256]{0:T(256)S(1)} %bitcast.605), kind=kOutput, calls=%fused_computation.4 | convolution fusion | flops 2419064832 | bytes 11810816 | tf_op jit(solution)/shard_map/dot_general | solution.py:182
  119.8 5.0 reshape.1011
  129.2 11.0 %convolution_convert_fusion.5 = bf16[256,3072]{1,0:T(8,128)(2,1)} fusion(bf16[1536,3072]{0,1:T(8,128)(2,1)} %bitcast.474, bf16[1,256,1536]{2,1,0:T(8,128)(2,1)S(1)} %copy-done.13, f32[1536]{0:T(1024)S(1)} %get-tuple-element.33, f32[1536]{0:T(1024)S(1)} %get-tuple-element.34, f32[256]{0:T(256)S(1)} %add_rsqrt_fusion.1, f32[256]{0:T(256)S(1)} %bitcast.607), kind=kOutput, calls=%fused_computation.5 | convolution fusion | flops 2419064832 | bytes 11810816 | tf_op jit(solution)/shard_map/dot_general | solution.py:182
  140.2 5.2 reshape.1009
  149.7 11.0 %convolution_convert_fusion.6 = bf16[256,3072]{1,0:T(8,128)(2,1)} fusion(bf16[1536,3072]{0,1:T(8,128)(2,1)} %bitcast.475, bf16[1,256,1536]{2,1,0:T(8,128)(2,1)S(1)} %copy-done.11, f32[1536]{0:T(1024)S(1)} %get-tuple-element.37, f32[1536]{0:T(1024)S(1)} %get-tuple-element.38, f32[256]{0:T(256)S(1)} %add_rsqrt_fusion.2, f32[256]{0:T(256)S(1)} %bitcast.609), kind=kOutput, calls=%fused_computation.6 | convolution fusion | flops 2419064832 | bytes 11810816 | tf_op jit(solution)/shard_map/dot_general | solution.py:182
  160.8 5.0 reshape.1007
  170.1 11.0 %convolution_convert_fusion.7 = bf16[256,3072]{1,0:T(8,128)(2,1)} fusion(bf16[1536,3072]{0,1:T(8,128)(2,1)} %bitcast.476, bf16[1,256,1536]{2,1,0:T(8,128)(2,1)S(1)} %copy-done.9, f32[1536]{0:T(1024)S(1)} %get-tuple-element.40, f32[1536]{0:T(1024)S(1)} %get-tuple-element.41, f32[256]{0:T(256)S(1)} %add_rsqrt_fusion.3, f32[256]{0:T(256)S(1)} %bitcast.603), kind=kOutput, calls=%fused_computation.7 | convolution fusion | flops 2419064832 | bytes 11810816 | tf_op jit(solution)/shard_map/dot_general | solution.py:182
  181.2 5.2 reshape.1005
  226.5 14.1 %collective-permute-done.22 = bf16[256,256]{1,0:T(8,128)(2,1)S(1)} collective-permute-done((bf16[256,256]{1,0:T(8,128)(2,1)}, bf16[256,256]{1,0:T(8,128)(2,1)S(1)}, u32[]{:S(2)}, u32[]{:S(2)}) %collective-permute-start.22) | collective-permute-done | bytes 131104 | tf_op jit(solution)/shard_map/ppermute | solution.py:111
  303.3 4.5 collective-permute-done.4
  317.5 8.4 %reduce-scatter.8.cloned.1.call-done = bf16[64,1536]{1,0:T(8,128)(2,1)} async-done(((bf16[256,1536]{1,0:T(8,128)(2,1)}), bf16[64,1536]{1,0:T(8,128)(2,1)}) %reduce-scatter.8.cloned.1.call-update) | async-done | bytes 196624 | tf_op jit(solution)/shard_map/reduce_scatter | solution.py:188
  325.9 24.8 %reduce-scatter.6.cloned.1.call-done = bf16[64,1536]{1,0:T(8,128)(2,1)} async-done(((bf16[256,1536]{1,0:T(8,128)(2,1)}), bf16[64,1536]{1,0:T(8,128)(2,1)}) %reduce-scatter.6.cloned.1.call-update) | async-done | bytes 196624 | tf_op jit(solution)/shard_map/reduce_scatter | solution.py:188
  388.3 4.3 collective-permute-done.45
  405.2 7.8 %convolution_convert_fusion = bf16[256,3072]{1,0:T(8,128)(2,1)S(1)} fusion(bf16[1536,3072]{1,0:T(8,128)(2,1)} %param.14, s32[]{:T(128)S(6)} %select_n.373, bf16[64,1536]{1,0:T(8,128)(2,1)S(1)} %collective-permute-done.55, bf16[64,1536]{1,0:T(8,128)(2,1)S(1)} %collective-permute-done.54, bf16[64,1536]{1,0:T(8,128)(2,1)} %copy-done.55, ...), kind=kOutput, calls=%fused_computation | convolution fusion | flops 2422996992 | bytes 11796484 | tf_op jit(solution)/shard_map/dot_general | solution.py:192
  414.1 7.7 %convolution_convert_fusion.1 = bf16[256,3072]{1,0:T(8,128)(2,1)S(1)} fusion(bf16[1536,3072]{1,0:T(8,128)(2,1)} %param.14, s32[]{:T(128)S(6)} %select_n.373, bf16[64,1536]{1,0:T(8,128)(2,1)S(1)} %collective-permute-done.46, bf16[64,1536]{1,0:T(8,128)(2,1)} %collective-permute-done.45, bf16[64,1536]{1,0:T(8,128)(2,1)S(1)} %copy-done.57, ...), kind=kOutput, calls=%fused_computation.1 | convolution fusion | flops 2422996992 | bytes 11796484 | tf_op jit(solution)/shard_map/dot_general | solution.py:192
  422.8 5.0 convolution_convert_fusion.2
  428.8 5.2 convolution_convert_fusion.3
  438.9 7.3 %collective-permute-done.57 = bf16[64,3072]{1,0:T(8,128)(2,1)S(1)} collective-permute-done((bf16[64,3072]{1,0:T(8,128)(2,1)S(1)}, bf16[64,3072]{1,0:T(8,128)(2,1)S(1)}, u32[]{:S(2)}, u32[]{:S(2)}) %collective-permute-start.57) | collective-permute-done | bytes 393248 | tf_op jit(solution)/shard_map/ppermute | solution.py:111
  446.2 8.4 %collective-permute-done.48 = bf16[64,3072]{1,0:T(8,128)(2,1)S(1)} collective-permute-done((bf16[64,3072]{1,0:T(8,128)(2,1)S(1)}, bf16[64,3072]{1,0:T(8,128)(2,1)S(1)}, u32[]{:S(2)}, u32[]{:S(2)}) %collective-permute-start.48) | collective-permute-done | bytes 393248 | tf_op jit(solution)/shard_map/ppermute | solution.py:111
  454.6 8.4 %collective-permute-done.39 = bf16[64,3072]{1,0:T(8,128)(2,1)S(1)} collective-permute-done((bf16[64,3072]{1,0:T(8,128)(2,1)S(1)}, bf16[64,3072]{1,0:T(8,128)(2,1)S(1)}, u32[]{:S(2)}, u32[]{:S(2)}) %collective-permute-start.39) | collective-permute-done | bytes 393248 | tf_op jit(solution)/shard_map/ppermute | solution.py:111
  463.1 8.0 %collective-permute-done.30 = bf16[64,3072]{1,0:T(8,128)(2,1)S(1)} collective-permute-done((bf16[64,3072]{1,0:T(8,128)(2,1)S(1)}, bf16[64,3072]{1,0:T(8,128)(2,1)S(1)}, u32[]{:S(2)}, u32[]{:S(2)}) %collective-permute-start.30) | collective-permute-done | bytes 393248 | tf_op jit(solution)/shard_map/ppermute | solution.py:111
  476.8 8.0 %collective-permute-done.31 = bf16[64,3072]{1,0:T(8,128)(2,1)S(1)} collective-permute-done((bf16[64,3072]{1,0:T(8,128)(2,1)S(1)}, bf16[64,3072]{1,0:T(8,128)(2,1)S(1)}, u32[]{:S(2)}, u32[]{:S(2)}) %collective-permute-start.31) | collective-permute-done | bytes 393248 | tf_op jit(solution)/shard_map/ppermute | solution.py:111
  485.0 8.2 %collective-permute-done.40 = bf16[64,3072]{1,0:T(8,128)(2,1)S(1)} collective-permute-done((bf16[64,3072]{1,0:T(8,128)(2,1)S(1)}, bf16[64,3072]{1,0:T(8,128)(2,1)S(1)}, u32[]{:S(2)}, u32[]{:S(2)}) %collective-permute-start.40) | collective-permute-done | bytes 393248 | tf_op jit(solution)/shard_map/ppermute | solution.py:111
  493.4 8.2 %collective-permute-done.49 = bf16[64,3072]{1,0:T(8,128)(2,1)S(1)} collective-permute-done((bf16[64,3072]{1,0:T(8,128)(2,1)S(1)}, bf16[64,3072]{1,0:T(8,128)(2,1)S(1)}, u32[]{:S(2)}, u32[]{:S(2)}) %collective-permute-start.49) | collective-permute-done | bytes 393248 | tf_op jit(solution)/shard_map/ppermute | solution.py:111
  501.9 6.9 %collective-permute-done.58 = bf16[64,3072]{1,0:T(8,128)(2,1)S(1)} collective-permute-done((bf16[64,3072]{1,0:T(8,128)(2,1)S(1)}, bf16[64,3072]{1,0:T(8,128)(2,1)S(1)}, u32[]{:S(2)}, u32[]{:S(2)}) %collective-permute-start.58) | collective-permute-done | bytes 393248 | tf_op jit(solution)/shard_map/ppermute | solution.py:111
  525.3 20.9 %reduce-scatter.14.cloned.1.call-done = bf16[64,1536]{1,0:T(8,128)(2,1)} async-done(((bf16[256,1536]{1,0:T(8,128)(2,1)}), bf16[64,1536]{1,0:T(8,128)(2,1)}) %reduce-scatter.14.cloned.1.call-update) | async-done | bytes 196624 | tf_op jit(solution)/shard_map/reduce_scatter | solution.py:201
  546.1 5.0 add_convert_fusion
  (422 shorter events, 221.8 us)
Async XLA Ops:
  6.5 310.9 %reduce-scatter.12.cloned.1.call-start = ((), (), s32[]{:S(2)}) async-start(), calls=%async_computation.8 | async-start | bytes 983040 | tf_op jit(solution)/shard_map/reduce_scatter | solution.py:188
  32.1 75.4 %collective-permute-start.18 = (f32[2,256]{1,0:T(2,128)S(1)}, f32[2,256]{1,0:T(2,128)S(1)}, u32[]{:S(2)}, u32[]{:S(2)}) collective-permute-start(f32[2,256]{1,0:T(2,128)S(1)} %pad_maximum_fusion.3), channel_id=1, source_target_pairs={{0,4},{4,0},{8,12},{12,8},{1,5},{5,1},{9,13},{13,9},{2,6},{6,2},{1... | collective-permute-start | bytes 6152 | tf_op jit(solution)/shard_map/ppermute | solution.py:111
  50.6 58.5 %collective-permute-start.12 = (f32[2,256]{1,0:T(2,128)S(1)}, f32[2,256]{1,0:T(2,128)S(1)}, u32[]{:S(2)}, u32[]{:S(2)}) collective-permute-start(f32[2,256]{1,0:T(2,128)S(1)} %pad_maximum_fusion.2), channel_id=1, source_target_pairs={{0,4},{4,0},{8,12},{12,8},{1,5},{5,1},{9,13},{13,9},{2,6},{6,2},{1... | collective-permute-start | bytes 6152 | tf_op jit(solution)/shard_map/ppermute | solution.py:111
  69.6 40.1 %collective-permute-start.6 = (f32[2,256]{1,0:T(2,128)S(1)}, f32[2,256]{1,0:T(2,128)S(1)}, u32[]{:S(2)}, u32[]{:S(2)}) collective-permute-start(f32[2,256]{1,0:T(2,128)S(1)} %pad_maximum_fusion.1), channel_id=1, source_target_pairs={{0,4},{4,0},{8,12},{12,8},{1,5},{5,1},{9,13},{13,9},{2,6},{6,2},{1... | collective-permute-start | bytes 6152 | tf_op jit(solution)/shard_map/ppermute | solution.py:111
  89.9 21.4 %collective-permute-start = (f32[2,256]{1,0:T(2,128)S(1)}, f32[2,256]{1,0:T(2,128)S(1)}, u32[]{:S(2)}, u32[]{:S(2)}) collective-permute-start(f32[2,256]{1,0:T(2,128)S(1)} %pad_maximum_fusion), channel_id=1, source_target_pairs={{0,4},{4,0},{8,12},{12,8},{1,5},{5,1},{9,13},{13,9},{2,6},{6,2},{1... | collective-permute-start | bytes 6152 | tf_op jit(solution)/shard_map/ppermute | solution.py:111
  109.1 19.8 %collective-permute-start.13 = (f32[2,256]{1,0:T(2,128)S(1)}, f32[2,256]{1,0:T(2,128)S(1)}, u32[]{:S(2)}, u32[]{:S(2)}) collective-permute-start(f32[2,256]{1,0:T(2,128)S(1)} %fusion.196), channel_id=1, source_target_pairs={{0,8},{4,12},{8,0},{12,4},{1,9},{5,13},{9,1},{13,5},{2,10},{6,14},... | collective-permute-start | bytes 6152 | tf_op jit(solution)/shard_map/ppermute | solution.py:111
  109.7 40.0 %collective-permute-start.7 = (f32[2,256]{1,0:T(2,128)S(1)}, f32[2,256]{1,0:T(2,128)S(1)}, u32[]{:S(2)}, u32[]{:S(2)}) collective-permute-start(f32[2,256]{1,0:T(2,128)S(1)} %fusion.197), channel_id=1, source_target_pairs={{0,8},{4,12},{8,0},{12,4},{1,9},{5,13},{9,1},{13,5},{2,10},{6,14},... | collective-permute-start | bytes 6152 | tf_op jit(solution)/shard_map/ppermute | solution.py:111
  111.3 58.8 %collective-permute-start.1 = (f32[2,256]{1,0:T(2,128)S(1)}, f32[2,256]{1,0:T(2,128)S(1)}, u32[]{:S(2)}, u32[]{:S(2)}) collective-permute-start(f32[2,256]{1,0:T(2,128)S(1)} %fusion.198), channel_id=1, source_target_pairs={{0,8},{4,12},{8,0},{12,4},{1,9},{5,13},{9,1},{13,5},{2,10},{6,14},... | collective-permute-start | bytes 6152 | tf_op jit(solution)/shard_map/ppermute | solution.py:111
  128.9 71.2 %collective-permute-start.20 = (bf16[2,3,256,256]{3,2,1,0:T(8,128)(2,1)}, bf16[2,3,256,256]{3,2,1,0:T(8,128)(2,1)}, u32[]{:S(2)}, u32[]{:S(2)}) collective-permute-start(bf16[2,3,256,256]{3,2,1,0:T(8,128)(2,1)} %bitcast.463), channel_id=1, source_target_pairs={{0,4},{4,0},{8,12},{12,8},{1,5},{5,1},{9,13},{13,9},{2,6},{6,2},{1... | collective-permute-start | bytes 2359304 | tf_op jit(solution)/shard_map/ppermute | solution.py:111
  149.4 53.3 %collective-permute-start.14 = (bf16[2,3,256,256]{3,2,1,0:T(8,128)(2,1)}, bf16[2,3,256,256]{3,2,1,0:T(8,128)(2,1)}, u32[]{:S(2)}, u32[]{:S(2)}) collective-permute-start(bf16[2,3,256,256]{3,2,1,0:T(8,128)(2,1)} %bitcast.464), channel_id=1, source_target_pairs={{0,4},{4,0},{8,12},{12,8},{1,5},{5,1},{9,13},{13,9},{2,6},{6,2},{1... | collective-permute-start | bytes 2359304 | tf_op jit(solution)/shard_map/ppermute | solution.py:111
  169.9 35.2 %collective-permute-start.8 = (bf16[2,3,256,256]{3,2,1,0:T(8,128)(2,1)}, bf16[2,3,256,256]{3,2,1,0:T(8,128)(2,1)}, u32[]{:S(2)}, u32[]{:S(2)}) collective-permute-start(bf16[2,3,256,256]{3,2,1,0:T(8,128)(2,1)} %bitcast.465), channel_id=1, source_target_pairs={{0,4},{4,0},{8,12},{12,8},{1,5},{5,1},{9,13},{13,9},{2,6},{6,2},{1... | collective-permute-start | bytes 2359304 | tf_op jit(solution)/shard_map/ppermute | solution.py:111
  189.6 18.8 %collective-permute-start.2 = (bf16[2,3,256,256]{3,2,1,0:T(8,128)(2,1)S(1)}, bf16[2,3,256,256]{3,2,1,0:T(8,128)(2,1)S(1)}, u32[]{:S(2)}, u32[]{:S(2)}) collective-permute-start(bf16[2,3,256,256]{3,2,1,0:T(8,128)(2,1)S(1)} %bitcast.525), channel_id=1, source_target_pairs={{0,4},{4,0},{8,12},{12,8},{1,5},{5,1},{9,13},{13,9},{2,6},{6,2},{1... | collective-permute-start | bytes 2359304 | tf_op jit(solution)/shard_map/ppermute | solution.py:111
  204.5 20.4 %collective-permute-start.15 = (bf16[3,256,256]{2,1,0:T(8,128)(2,1)}, bf16[3,256,256]{2,1,0:T(8,128)(2,1)}, u32[]{:S(2)}, u32[]{:S(2)}) collective-permute-start(bf16[3,256,256]{2,1,0:T(8,128)(2,1)} %fusion.128), channel_id=1, source_target_pairs={{0,8},{4,12},{8,0},{12,4},{1,9},{5,13},{9,1},{13,5},{2,10},{6,14},... | collective-permute-start | bytes 1179656 | tf_op jit(solution)/shard_map/ppermute | solution.py:111
  206.9 53.3 %collective-permute-start.9 = (bf16[3,256,256]{2,1,0:T(8,128)(2,1)}, bf16[3,256,256]{2,1,0:T(8,128)(2,1)}, u32[]{:S(2)}, u32[]{:S(2)}) collective-permute-start(bf16[3,256,256]{2,1,0:T(8,128)(2,1)} %fusion.131), channel_id=1, source_target_pairs={{0,8},{4,12},{8,0},{12,4},{1,9},{5,13},{9,1},{13,5},{2,10},{6,14},... | collective-permute-start | bytes 1179656 | tf_op jit(solution)/shard_map/ppermute | solution.py:111
  209.4 73.8 %collective-permute-start.3 = (bf16[3,256,256]{2,1,0:T(8,128)(2,1)}, bf16[3,256,256]{2,1,0:T(8,128)(2,1)}, u32[]{:S(2)}, u32[]{:S(2)}) collective-permute-start(bf16[3,256,256]{2,1,0:T(8,128)(2,1)} %fusion.134), channel_id=1, source_target_pairs={{0,8},{4,12},{8,0},{12,4},{1,9},{5,13},{9,1},{13,5},{2,10},{6,14},... | collective-permute-start | bytes 1179656 | tf_op jit(solution)/shard_map/ppermute | solution.py:111
  222.6 18.0 %collective-permute-start.22 = (bf16[256,256]{1,0:T(8,128)(2,1)}, bf16[256,256]{1,0:T(8,128)(2,1)S(1)}, u32[]{:S(2)}, u32[]{:S(2)}) collective-permute-start(bf16[256,256]{1,0:T(8,128)(2,1)} %copy.101), channel_id=1, source_target_pairs={{0,8},{4,12},{8,0},{12,4},{1,9},{5,13},{9,1},{13,5},{2,10},{6,14},... | collective-permute-start | bytes 393224 | tf_op jit(solution)/shard_map/ppermute | solution.py:111
  252.9 64.6 %reduce-scatter.10.cloned.1.call-start = ((), (), s32[]{:S(2)}) async-start(), calls=%async_computation.7 | async-start | bytes 983040 | tf_op jit(solution)/shard_map/reduce_scatter | solution.py:188
  275.8 50.1 %reduce-scatter.8.cloned.1.call-start = ((), (), s32[]{:S(2)}) async-start(), calls=%async_computation.6 | async-start | bytes 983040 | tf_op jit(solution)/shard_map/reduce_scatter | solution.py:188
  299.8 50.9 %reduce-scatter.6.cloned.1.call-start = ((), (), s32[]{:S(2)}) async-start(), calls=%async_computation.5 | async-start | bytes 983040 | tf_op jit(solution)/shard_map/reduce_scatter | solution.py:188
  317.4 228.7 %reduce-scatter.14.cloned.1.call-start = ((), (), s32[]{:S(2)}) async-start(), calls=%async_computation.9 | async-start | bytes 983040 | tf_op jit(solution)/shard_map/reduce_scatter | solution.py:201
  365.1 19.0 %collective-permute-start.26 = (bf16[64,1536]{1,0:T(8,128)(2,1)S(1)}, bf16[64,1536]{1,0:T(8,128)(2,1)S(1)}, u32[]{:S(2)}, u32[]{:S(2)}) collective-permute-start(bf16[64,1536]{1,0:T(8,128)(2,1)S(1)} %get-tuple-element.52), channel_id=1, source_target_pairs={{0,1},{1,2},{2,3},{3,0},{4,5},{5,6},{6,7},{7,4},{8,9},{9,10},{10,1... | collective-permute-start | bytes 589832 | tf_op jit(solution)/shard_map/ppermute | solution.py:15
  392.6 20.6 %collective-permute-start.46 = (bf16[64,1536]{1,0:T(8,128)(2,1)}, bf16[64,1536]{1,0:T(8,128)(2,1)S(1)}, u32[]{:S(2)}, u32[]{:S(2)}) collective-permute-start(bf16[64,1536]{1,0:T(8,128)(2,1)} %collective-permute-done.45), channel_id=1, source_target_pairs={{0,1},{1,2},{2,3},{3,0},{4,5},{5,6},{6,7},{7,4},{8,9},{9,10},{10,1... | collective-permute-start | bytes 589832 | tf_op jit(solution)/shard_map/ppermute | solution.py:15
  396.9 25.1 %collective-permute-start.37 = (bf16[64,1536]{1,0:T(8,128)(2,1)}, bf16[64,1536]{1,0:T(8,128)(2,1)S(1)}, u32[]{:S(2)}, u32[]{:S(2)}) collective-permute-start(bf16[64,1536]{1,0:T(8,128)(2,1)} %collective-permute-done.36), channel_id=1, source_target_pairs={{0,1},{1,2},{2,3},{3,0},{4,5},{5,6},{6,7},{7,4},{8,9},{9,10},{10,1... | collective-permute-start | bytes 589832 | tf_op jit(solution)/shard_map/ppermute | solution.py:15
  401.1 26.9 %collective-permute-start.28 = (bf16[64,1536]{1,0:T(8,128)(2,1)}, bf16[64,1536]{1,0:T(8,128)(2,1)S(1)}, u32[]{:S(2)}, u32[]{:S(2)}) collective-permute-start(bf16[64,1536]{1,0:T(8,128)(2,1)} %collective-permute-done.27), channel_id=1, source_target_pairs={{0,1},{1,2},{2,3},{3,0},{4,5},{5,6},{6,7},{7,4},{8,9},{9,10},{10,1... | collective-permute-start | bytes 589832 | tf_op jit(solution)/shard_map/ppermute | solution.py:15
  413.1 21.0 %collective-permute-start.56 = (bf16[2,64,3072]{2,1,0:T(8,128)(2,1)S(1)}, bf16[2,64,3072]{2,1,0:T(8,128)(2,1)S(1)}, u32[]{:S(2)}, u32[]{:S(2)}) collective-permute-start(bf16[2,64,3072]{2,1,0:T(8,128)(2,1)S(1)} %dynamic-slice_bitcast_fusion), channel_id=1, source_target_pairs={{0,4},{4,0},{8,12},{12,8},{1,5},{5,1},{9,13},{13,9},{2,6},{6,2},{1... | collective-permute-start | bytes 2359304 | tf_op jit(solution)/shard_map/ppermute | solution.py:111
  435.0 19.7 %collective-permute-start.48 = (bf16[64,3072]{1,0:T(8,128)(2,1)S(1)}, bf16[64,3072]{1,0:T(8,128)(2,1)S(1)}, u32[]{:S(2)}, u32[]{:S(2)}) collective-permute-start(bf16[64,3072]{1,0:T(8,128)(2,1)S(1)} %fusion.116), channel_id=1, source_target_pairs={{0,8},{4,12},{8,0},{12,4},{1,9},{5,13},{9,1},{13,5},{2,10},{6,14},... | collective-permute-start | bytes 1179656 | tf_op jit(solution)/shard_map/ppermute | solution.py:111
  436.6 26.5 %collective-permute-start.39 = (bf16[64,3072]{1,0:T(8,128)(2,1)S(1)}, bf16[64,3072]{1,0:T(8,128)(2,1)S(1)}, u32[]{:S(2)}, u32[]{:S(2)}) collective-permute-start(bf16[64,3072]{1,0:T(8,128)(2,1)S(1)} %fusion.119), channel_id=1, source_target_pairs={{0,8},{4,12},{8,0},{12,4},{1,9},{5,13},{9,1},{13,5},{2,10},{6,14},... | collective-permute-start | bytes 1179656 | tf_op jit(solution)/shard_map/ppermute | solution.py:111
  437.3 33.8 %collective-permute-start.30 = (bf16[64,3072]{1,0:T(8,128)(2,1)S(1)}, bf16[64,3072]{1,0:T(8,128)(2,1)S(1)}, u32[]{:S(2)}, u32[]{:S(2)}) collective-permute-start(bf16[64,3072]{1,0:T(8,128)(2,1)S(1)} %fusion.122), channel_id=1, source_target_pairs={{0,8},{4,12},{8,0},{12,4},{1,9},{5,13},{9,1},{13,5},{2,10},{6,14},... | collective-permute-start | bytes 1179656 | tf_op jit(solution)/shard_map/ppermute | solution.py:111
  473.3 19.9 %collective-permute-start.40 = (bf16[64,3072]{1,0:T(8,128)(2,1)S(1)}, bf16[64,3072]{1,0:T(8,128)(2,1)S(1)}, u32[]{:S(2)}, u32[]{:S(2)}) collective-permute-start(bf16[64,3072]{1,0:T(8,128)(2,1)S(1)} %get-tuple-element.73), channel_id=1, source_target_pairs={{0,8},{4,12},{8,0},{12,4},{1,9},{5,13},{9,1},{13,5},{2,10},{6,14},... | collective-permute-start | bytes 1179656 | tf_op jit(solution)/shard_map/ppermute | solution.py:111
  474.8 26.9 %collective-permute-start.49 = (bf16[64,3072]{1,0:T(8,128)(2,1)S(1)}, bf16[64,3072]{1,0:T(8,128)(2,1)S(1)}, u32[]{:S(2)}, u32[]{:S(2)}) collective-permute-start(bf16[64,3072]{1,0:T(8,128)(2,1)S(1)} %get-tuple-element.74), channel_id=1, source_target_pairs={{0,8},{4,12},{8,0},{12,4},{1,9},{5,13},{9,1},{13,5},{2,10},{6,14},... | collective-permute-start | bytes 1179656 | tf_op jit(solution)/shard_map/ppermute | solution.py:111
  475.4 33.4 %collective-permute-start.58 = (bf16[64,3072]{1,0:T(8,128)(2,1)S(1)}, bf16[64,3072]{1,0:T(8,128)(2,1)S(1)}, u32[]{:S(2)}, u32[]{:S(2)}) collective-permute-start(bf16[64,3072]{1,0:T(8,128)(2,1)S(1)} %get-tuple-element.75), channel_id=1, source_target_pairs={{0,8},{4,12},{8,0},{12,4},{1,9},{5,13},{9,1},{13,5},{2,10},{6,14},... | collective-permute-start | bytes 1179656 | tf_op jit(solution)/shard_map/ppermute | solution.py:111
  484.9 26.7 %collective-permute-start.32 = (bf16[2,64,3072]{2,1,0:T(8,128)(2,1)S(1)}, bf16[2,64,3072]{2,1,0:T(8,128)(2,1)S(1)}, u32[]{:S(2)}, u32[]{:S(2)}) collective-permute-start(bf16[2,64,3072]{2,1,0:T(8,128)(2,1)S(1)} %maximum_select_fusion.4), channel_id=1, source_target_pairs={{0,4},{4,0},{8,12},{12,8},{1,5},{5,1},{9,13},{13,9},{2,6},{6,2},{1... | collective-permute-start | bytes 2359304 | tf_op jit(solution)/shard_map/ppermute | solution.py:111
  (98 other events, 1679.9 us)
Sparse Core Ops, SparseCore 0:
  253.0 23.1 reduce-scatter.11
  278.4 22.5 reduce-scatter.9
  303.3 22.5 reduce-scatter.7
  328.1 22.5 reduce-scatter.5
  525.4 20.7 reduce-scatter.13
